TPU v7x, 1024 devices: a whole 8x8x8 slice. The times are simulated.
1024 devices in a mesh: blk: 32 (over y, z_lo), ulysses: 32 (over z_hi, x, core).
Axes of the slice: x: 8, y: 8, z: 8 (z_hi: 2, z_lo: 4; z = z_hi * 4 + z_lo), core: 2. Of those that a mesh axis runs over, the one named last changes fastest.
Arguments:
- queries: bfloat16 [6144, 4096], P(('blk', 'ulysses')), may hold values from -8 to 8
- key_vectors: bfloat16 [6144, 4096], P(('blk', 'ulysses')), may hold values from -8 to 8
- value_vectors: bfloat16 [6144, 4096], P(('blk', 'ulysses')), may hold values from -12 to 12
- cotangent: bfloat16 [6144, 4096], P(('blk', 'ulysses')), may hold values from -192 to 192
Outputs:
- grad_queries: bfloat16 [6144, 4096], P(('blk', 'ulysses'))
- grad_keys: bfloat16 [6144, 4096], P(('blk', 'ulysses'))
- grad_values: bfloat16 [6144, 4096], P(('blk', 'ulysses'))
All inputs are finite; a program needn't handle non-finite values.
Results may differ from a plain program's by a relative error of at most 0.0067.
Values may be sent and summed in bfloat16 or wider, within the bound.
A program may use at most 64 MiB of HBM per device.

v0:
```python
import math

import jax
import jax.numpy as jnp
from jax import lax
from jax.sharding import PartitionSpec as P

HEADS = 32
D_HEAD = 128


def scores(query_part, key_part, score_scale):
    return (
        jnp.einsum("qhd,khd->hqk", query_part, key_part, preferred_element_type=jnp.float32)
        * score_scale
    )


def local(queries, key_vectors, value_vectors, cotangent):
    ulysses_size = lax.axis_size("ulysses")
    head_dev = HEADS // ulysses_size
    score_scale = 1.0 / math.sqrt(D_HEAD)
    query_heads, key_heads, value_heads, grad_heads = (
        lax.all_to_all(queries, "ulysses", split_axis=1, concat_axis=0, tiled=True),
        lax.all_to_all(key_vectors, "ulysses", split_axis=1, concat_axis=0, tiled=True),
        lax.all_to_all(value_vectors, "ulysses", split_axis=1, concat_axis=0, tiled=True),
        lax.all_to_all(cotangent, "ulysses", split_axis=1, concat_axis=0, tiled=True),
    )
    local_rows = query_heads.shape[0]

    def split_heads(matrix):
        return matrix.reshape(matrix.shape[0], head_dev, D_HEAD)

    own_query = split_heads(query_heads)
    own_key = split_heads(key_heads)
    own_value = split_heads(value_heads)
    own_grad = split_heads(grad_heads)
    held_key, held_value = (
        lax.all_gather(key_heads, "blk", axis=0, tiled=True),
        lax.all_gather(value_heads, "blk", axis=0, tiled=True),
    )
    held_key = split_heads(held_key)
    held_value = split_heads(held_value)
    logits = scores(own_query, held_key, score_scale)
    grad_weights = jnp.einsum(
        "qhd,khd->hqk", own_grad, held_value, preferred_element_type=jnp.float32
    )
    block_top = jnp.max(logits, axis=2)
    exp_terms = jnp.exp(logits - block_top[:, :, None])
    row_total = jnp.sum(exp_terms, axis=2)
    row_sum = jnp.sum(exp_terms * grad_weights, axis=2)
    log_total = block_top + jnp.log(row_total)
    row_dot = row_sum / row_total
    all_log, all_dot = (
        lax.all_gather(log_total.T, "blk", axis=0, tiled=True),
        lax.all_gather(row_dot.T, "blk", axis=0, tiled=True),
    )
    logits = scores(own_query, held_key, score_scale)
    weights = jnp.exp(logits - log_total[:, :, None])
    grad_weights = jnp.einsum(
        "qhd,khd->hqk", own_grad, held_value, preferred_element_type=jnp.float32
    )
    grad_low = (weights * (grad_weights - row_dot[:, :, None])).astype(jnp.bfloat16)
    grad_query = jnp.einsum("hqk,khd->qhd", grad_low, held_key, preferred_element_type=jnp.float32)
    remote_query = split_heads(lax.all_gather(query_heads, "blk", axis=0, tiled=True))
    remote_grad = split_heads(lax.all_gather(grad_heads, "blk", axis=0, tiled=True))
    logits = scores(remote_query, own_key, score_scale)
    weights = jnp.exp(logits - all_log.T[:, :, None])
    grad_weights = jnp.einsum(
        "qhd,khd->hqk", remote_grad, own_value, preferred_element_type=jnp.float32
    )
    grad_low = (weights * (grad_weights - all_dot.T[:, :, None])).astype(jnp.bfloat16)
    weights_low = weights.astype(jnp.bfloat16)
    grad_key = jnp.einsum(
        "hqk,qhd->khd", grad_low, remote_query, preferred_element_type=jnp.float32
    )
    grad_value = jnp.einsum(
        "hqk,qhd->khd", weights_low, remote_grad, preferred_element_type=jnp.float32
    )
    grad_key, grad_value = (grad_key, grad_value)

    def to_rows(summed, factor):
        return (summed * factor).astype(jnp.bfloat16).reshape(local_rows, head_dev * D_HEAD)

    return (
        lax.all_to_all(
            to_rows(grad_query, score_scale), "ulysses", split_axis=0, concat_axis=1, tiled=True
        ),
        lax.all_to_all(
            to_rows(grad_key, score_scale), "ulysses", split_axis=0, concat_axis=1, tiled=True
        ),
        lax.all_to_all(
            to_rows(grad_value, 1.0), "ulysses", split_axis=0, concat_axis=1, tiled=True
        ),
    )


def solution(mesh):
    placed = (
        P(("blk", "ulysses"), None),
        P(("blk", "ulysses"), None),
        P(("blk", "ulysses"), None),
        P(("blk", "ulysses"), None),
    )
    return jax.shard_map(
        local,
        mesh=mesh,
        in_specs=placed,
        out_specs=(
            P(("blk", "ulysses"), None),
            P(("blk", "ulysses"), None),
            P(("blk", "ulysses"), None),
        ),
        check_vma=False,
    )
```

profile of v0, /device:TPU:1, one launch (start us, length us, event | category | flops | bytes accessed | tf_op | source)
XLA Modules:
  0.0 731.6 jit_solution(14645888023038799026)
XLA Ops:
  7.2 0.0 all-gather.7.cloned.1.call-start
  7.2 32.5 %all_to_all.127 = bf16[6,32,128]{2,0,1:T(8,128)(2,1)S(1)} all-to-all(bf16[6,32,128]{2,0,1:T(8,128)(2,1)} %bitcast.60), channel_id=1, replica_groups=mesh['blk'=32,'ulysses'=32] {'ulysses'}, dimensions={1} | all-to-all | bytes 98304 | tf_op jit(solution)/shard_map/all_to_all | solution.py:25
  39.7 0.6 all_to_all.100
  40.4 0.0 all-gather.7.cloned.1.call-update
  40.4 0.0 all-gather.9.cloned.1.call-start
  40.4 16.8 %all_to_all.128 = bf16[6,32,128]{2,0,1:T(8,128)(2,1)S(1)} all-to-all(bf16[6,32,128]{2,0,1:T(8,128)(2,1)} %bitcast.61), channel_id=1, replica_groups=mesh['blk'=32,'ulysses'=32] {'ulysses'}, dimensions={1} | all-to-all | bytes 98304 | tf_op jit(solution)/shard_map/all_to_all | solution.py:26
  57.3 0.6 all_to_all.107
  57.9 0.0 all-gather.9.cloned.1.call-update
  57.9 0.0 all-gather.11.cloned.1.call-start
  58.0 16.8 %all_to_all.129 = bf16[6,32,128]{2,0,1:T(8,128)(2,1)S(1)} all-to-all(bf16[6,32,128]{2,0,1:T(8,128)(2,1)} %bitcast.62), channel_id=1, replica_groups=mesh['blk'=32,'ulysses'=32] {'ulysses'}, dimensions={1} | all-to-all | bytes 98304 | tf_op jit(solution)/shard_map/all_to_all | solution.py:24
  74.8 0.6 reshape.178
  75.4 0.0 all-gather.11.cloned.1.call-update
  75.5 0.0 all-gather.13.cloned.1.call-start
  75.5 16.8 %all_to_all.130 = bf16[6,32,128]{2,0,1:T(8,128)(2,1)S(1)} all-to-all(bf16[6,32,128]{2,0,1:T(8,128)(2,1)} %bitcast.63), channel_id=1, replica_groups=mesh['blk'=32,'ulysses'=32] {'ulysses'}, dimensions={1} | all-to-all | bytes 98304 | tf_op jit(solution)/shard_map/all_to_all | solution.py:27
  92.3 0.6 reshape.179
  93.0 0.0 copy-start.6
  93.0 0.0 all-gather.13.cloned.1.call-update
  93.0 1.3 dynamic-slice
  94.9 79.5 %all-gather.7.cloned.1.call-done = bf16[6144,128]{1,0:T(8,128)(2,1)} async-done(((bf16[192,128]{1,0:T(8,128)(2,1)}), bf16[6144,128]{1,0:T(8,128)(2,1)}) %all-gather.7.cloned.1.call-update) | async-done | bytes 1572880 | tf_op jit(solution)/shard_map/all_gather | solution.py:39
  174.5 4.3 fusion.23
  178.8 155.4 %all-gather.9.cloned.1.call-done = bf16[6144,128]{1,0:T(8,128)(2,1)} async-done(((bf16[192,128]{1,0:T(8,128)(2,1)}), bf16[6144,128]{1,0:T(8,128)(2,1)}) %all-gather.9.cloned.1.call-update) | async-done | bytes 1572880 | tf_op jit(solution)/shard_map/all_gather | solution.py:40
  334.2 0.0 copy-done.6
  334.2 0.0 copy-start
  334.2 0.0 copy-start.2
  334.2 4.3 fusion.4
  338.5 0.1 fusion.22
  338.7 0.1 fusion.21
  338.8 0.0 copy-done
  338.8 0.1 copy-done.2
  338.9 0.0 copy-start.4
  338.9 1.4 fusion.20
  340.3 0.7 all_to_all.108
  340.9 33.8 %all-to-all-start.4 = ((bf16[32,6,128]{2,1,0:T(8,128)(2,1)}), bf16[32,6,128]{2,1,0:T(8,128)(2,1)S(1)}, u32[]{:S(2)}, u32[]{:S(2)}) async-start(bf16[32,6,128]{2,1,0:T(8,128)(2,1)} %all_to_all.108), calls=%async_computation.4 | async-start | bytes 131072 | tf_op jit(solution)/shard_map/all_to_all | solution.py:86
  374.8 127.6 %all-reduce.2 = (f32[6144]{0:T(1024)S(1)}, f32[6144]{0:T(1024)S(1)}) all-reduce(f32[6144]{0:T(1024)S(1)} %get-tuple-element.9, f32[6144]{0:T(1024)S(1)} %get-tuple-element.7), channel_id=2, replica_groups=mesh['blk'=32,'ulysses'=32] {'blk'}, use_global_device_ids=true, to_apply=%add | all-reduce | flops 12288 | bytes 98304
  502.4 0.0 all-gather.11.cloned.1.call-done
  502.4 0.0 copy-done.4
  502.4 0.0 copy-start.1
  502.4 0.0 copy-start.5
  502.4 4.5 fusion.2
  506.9 148.6 %all-gather.13.cloned.1.call-done = bf16[6144,128]{1,0:T(8,128)(2,1)} async-done(((bf16[192,128]{1,0:T(8,128)(2,1)}), bf16[6144,128]{1,0:T(8,128)(2,1)}) %all-gather.13.cloned.1.call-update) | async-done | bytes 1572880 | tf_op jit(solution)/shard_map/all_gather | solution.py:66
  655.5 0.0 copy-start.3
  655.5 0.0 copy-done.1
  655.5 0.0 copy-done.5
  655.5 4.3 fusion.19
  659.8 0.7 all_to_all.112
  660.5 0.0 all-to-all-done.4
  660.5 33.8 %all-to-all-start.5 = ((bf16[32,6,128]{2,1,0:T(8,128)(2,1)}), bf16[32,6,128]{2,1,0:T(8,128)(2,1)S(1)}, u32[]{:S(2)}, u32[]{:S(2)}) async-start(bf16[32,6,128]{2,1,0:T(8,128)(2,1)} %all_to_all.112), calls=%async_computation.5 | async-start | bytes 131072 | tf_op jit(solution)/shard_map/all_to_all | solution.py:89
  694.3 0.0 copy-done.3
  694.3 3.1 fusion.16
  697.4 0.7 all_to_all.116
  698.1 8.2 %all-to-all-done.5 = bf16[32,6,128]{2,1,0:T(8,128)(2,1)S(1)} async-done(((bf16[32,6,128]{2,1,0:T(8,128)(2,1)}), bf16[32,6,128]{2,1,0:T(8,128)(2,1)S(1)}, u32[]{:S(2)}, u32[]{:S(2)}) %all-to-all-start.5) | async-done | bytes 49184 | tf_op jit(solution)/shard_map/all_to_all | solution.py:89
  706.3 4.8 all-to-all-start.6
  711.1 12.1 %all-to-all-done.6 = bf16[32,6,128]{2,1,0:T(8,128)(2,1)S(1)} async-done(((bf16[32,6,128]{2,1,0:T(8,128)(2,1)}), bf16[32,6,128]{2,1,0:T(8,128)(2,1)S(1)}, u32[]{:S(2)}, u32[]{:S(2)}) %all-to-all-start.6) | async-done | bytes 49184 | tf_op jit(solution)/shard_map/all_to_all | solution.py:92
  723.2 0.6 copy.16
  723.8 0.6 copy.17
  724.4 0.6 copy.18
  (2 shorter events, 0.0 us)
Async XLA Ops:
  7.2 167.3 %all-gather.7.cloned.1.call-start = ((), (), s32[]{:S(2)}) async-start(), calls=%async_computation.7 | async-start | bytes 1622016 | tf_op jit(solution)/shard_map/all_gather | solution.py:39
  40.4 293.8 %all-gather.9.cloned.1.call-start = ((), (), s32[]{:S(2)}) async-start(), calls=%async_computation.8 | async-start | bytes 1622016 | tf_op jit(solution)/shard_map/all_gather | solution.py:40
  57.9 444.5 %all-gather.11.cloned.1.call-start = ((), (), s32[]{:S(2)}) async-start(), calls=%async_computation.9 | async-start | bytes 1622016 | tf_op jit(solution)/shard_map/all_gather | solution.py:65
  75.5 580.0 %all-gather.13.cloned.1.call-start = ((), (), s32[]{:S(2)}) async-start(), calls=%async_computation.10 | async-start | bytes 1622016 | tf_op jit(solution)/shard_map/all_gather | solution.py:66
  93.0 241.2 %copy-start.6 = (bf16[192,128]{1,0:T(8,128)(2,1)S(1)}, bf16[192,128]{1,0:T(8,128)(2,1)}, u32[]{:S(2)}) copy-start(bf16[192,128]{1,0:T(8,128)(2,1)} %reshape.179) | copy-start | bytes 147460
  334.2 4.6 copy-start
  334.2 4.7 copy-start.2
  338.9 163.5 %copy-start.4 = (bf16[192,128]{1,0:T(8,128)(2,1)S(1)}, bf16[192,128]{1,0:T(8,128)(2,1)}, u32[]{:S(2)}) copy-start(bf16[192,128]{1,0:T(8,128)(2,1)} %all_to_all.100) | copy-start | bytes 147460
  340.9 319.5 %all-to-all-start.4 = ((bf16[32,6,128]{2,1,0:T(8,128)(2,1)}), bf16[32,6,128]{2,1,0:T(8,128)(2,1)S(1)}, u32[]{:S(2)}, u32[]{:S(2)}) async-start(bf16[32,6,128]{2,1,0:T(8,128)(2,1)} %all_to_all.108), calls=%async_computation.4 | async-start | bytes 131072 | tf_op jit(solution)/shard_map/all_to_all | solution.py:86
  502.4 153.1 %copy-start.1 = (bf16[6144,128]{1,0:T(8,128)(2,1)S(1)}, bf16[6144,128]{1,0:T(8,128)(2,1)}, u32[]{:S(2)}) copy-start(bf16[6144,128]{1,0:T(8,128)(2,1)} %all-gather.11.cloned.1.call-done) | copy-start | bytes 4718596
  502.4 153.1 %copy-start.5 = (bf16[192,128]{1,0:T(8,128)(2,1)S(1)}, bf16[192,128]{1,0:T(8,128)(2,1)}, u32[]{:S(2)}) copy-start(bf16[192,128]{1,0:T(8,128)(2,1)} %all_to_all.107) | copy-start | bytes 147460
  655.5 38.8 %copy-start.3 = (bf16[6144,128]{1,0:T(8,128)(2,1)S(1)}, bf16[6144,128]{1,0:T(8,128)(2,1)}, u32[]{:S(2)}) copy-start(bf16[6144,128]{1,0:T(8,128)(2,1)} %all-gather.13.cloned.1.call-done) | copy-start | bytes 4718596
  660.5 45.8 %all-to-all-start.5 = ((bf16[32,6,128]{2,1,0:T(8,128)(2,1)}), bf16[32,6,128]{2,1,0:T(8,128)(2,1)S(1)}, u32[]{:S(2)}, u32[]{:S(2)}) async-start(bf16[32,6,128]{2,1,0:T(8,128)(2,1)} %all_to_all.112), calls=%async_computation.5 | async-start | bytes 131072 | tf_op jit(solution)/shard_map/all_to_all | solution.py:89
  706.3 16.8 %all-to-all-start.6 = ((bf16[32,6,128]{2,1,0:T(8,128)(2,1)}), bf16[32,6,128]{2,1,0:T(8,128)(2,1)S(1)}, u32[]{:S(2)}, u32[]{:S(2)}) async-start(bf16[32,6,128]{2,1,0:T(8,128)(2,1)} %all_to_all.116), calls=%async_computation.6 | async-start | bytes 131072 | tf_op jit(solution)/shard_map/all_to_all | solution.py:92
Sparse Core Ops, SparseCore 0:
  40.5 133.9 all-gather.6
  177.1 157.0 all-gather.8
  337.4 158.0 all-gather.10
  498.0 157.4 all-gather.12
where the time goes:
time: 732 us
  waiting for transfers between devices  404 us (55%)
  blocking collectives  211 us (29%)
  starting transfers between devices  72.6 us (10%)
  matrix products  22 us (3%)
  between operations  14.5 us (2%)
  local copies, waits for them, and re-layouts  7.76 us (1%)
    all_gather x1, waiting for transfers between devices, local(): lax.all_gather(value_heads, 'blk', axis=0, tiled=True)  155 us
    all_gather x1, waiting for transfers between devices, local(): lax.all_gather(grad_heads, 'blk', axis=0, tiled=True)  149 us
    unnamed x1, blocking collectives  128 us
    all_gather x1, waiting for transfers between devices, local(): lax.all_gather(key_heads, 'blk', axis=0, tiled=True)  79.5 us
    all_to_all x1, starting transfers between devices, local(): lax.all_to_all(to_rows(grad_key, score_scale), 'ulysses', split_axis=0, c...  33.8 us
    all_to_all x1, starting transfers between devices, local(): lax.all_to_all(to_rows(grad_query, score_scale), 'ulysses', split_axis=0,...  33.8 us
    all_to_all x1, blocking collectives, local(): lax.all_to_all(key_vectors, 'ulysses', split_axis=1, concat_axis=0, tiled...  32.5 us
    all_to_all x1, blocking collectives, local(): lax.all_to_all(queries, 'ulysses', split_axis=1, concat_axis=0, tiled=True)  16.8 us
  transfers between devices with their start and end apart: 7, of which 5 were waited for; matrix products, arithmetic and copies ran while one was open for 3% of the time, Pallas kernels for 0%

commit v1 on v0

v1 whole, which is shorter than its diff:
```python
import functools
import math

import jax
import jax.numpy as jnp
import numpy as np
from jax import lax
from jax.experimental import pallas as pl
from jax.experimental.pallas import tpu as pltpu
from jax.sharding import PartitionSpec as P

D = 128
NQ = 8
NK = 4
NP = NQ // 2
F32 = jnp.float32
BF16 = jnp.bfloat16
GROUP = 8


def dot_nt(a, b):
    return lax.dot_general(a, b, (((1,), (1,)), ((), ())), preferred_element_type=F32)


def log2(x):
    return jnp.log(x) * (1.0 / math.log(2.0))


def q_mask(k):
    return (k >> 1) & 1, (k & 1) | ((k >> 2) & 1) << 1


def k_mask(j):
    return (j & 1) << 2 | (j >> 1) << 1, 0


def h_mask(i):
    iz, ix, iy = i >> 4, (i >> 2) & 3, i & 3
    mb = iy << 3 | (4 if iy == 2 else 0) | (3 if iz else 0)
    mu = iz << 4 | ix << 2 | (2 if ix == 2 else 0)
    return mb, mu


def kernel(
    nu, t, q_hbm, k_hbm, v_hbm, g_hbm, sort_hbm, unsort_hbm, dq_ref, dk_ref, dv_ref,
    stage, sort_ref, unsort_ref, sbuf, rbuf, qg, kv, e_s, gw_s, gl_s, mlr, fin, st_send, st_all,
    dq_send, dq_recv, dkv_send, dkv_recv, osend, orecv,
    stage_sem, sort_sem, a2a_send, a2a_recv, kv_ssem, kv_rsem, qg_ssem, qg_rsem,
    st_ssem, st_rsem, dq_ssem, dq_rsem, dkv_ssem, dkv_rsem, out_send, out_recv,
):
    rows = nu * t
    cols = 2 * rows
    pack = 4 * t
    u = lax.axis_index("ulysses")
    blk = lax.axis_index("blk")
    scale = 1.0 / math.sqrt(D)
    scale2 = scale * math.log2(math.e)

    def flips(value):
        return [(1 - 2 * ((value // (1 << b)) % 2)) * (1 << b) for b in range(5)]

    def flipped(value, flip, mask):
        for b in range(5):
            if mask >> b & 1:
                value = value + flip[b]
        return value

    blk_flip, u_flip = flips(blk), flips(u)
    head = (u // 16) * 16 + ((u // 4) % 4) * 4 + blk // 8
    head_flip = flips(head)

    def peer(masks):
        return {"blk": flipped(blk, blk_flip, masks[0]), "ulysses": flipped(u, u_flip, masks[1])}

    def remote(src, dst, ssem, rsem, masks):
        return pltpu.make_async_remote_copy(
            src_ref=src, dst_ref=dst, send_sem=ssem, recv_sem=rsem,
            device_id=peer(masks), device_id_type=pl.DeviceIdType.MESH,
        )

    loads = [
        pltpu.make_async_copy(src, stage.at[a], stage_sem.at[a])
        for a, src in enumerate((q_hbm, k_hbm, v_hbm, g_hbm))
    ]
    loads.append(pltpu.make_async_copy(sort_hbm, sort_ref, sort_sem.at[0]))
    loads.append(pltpu.make_async_copy(unsort_hbm, unsort_ref, sort_sem.at[1]))
    for c in loads:
        c.start()

    barrier = pltpu.get_barrier_semaphore()
    partners = [h_mask(i) for i in range(1, nu)]
    partners += [q_mask(k) for k in range(1, NQ)] + [k_mask(j) for j in range(1, NK)]
    for masks in partners:
        pl.semaphore_signal(
            barrier, inc=1, device_id=peer(masks), device_id_type=pl.DeviceIdType.MESH
        )

    for c in loads:
        c.wait()
    packed = jnp.concatenate([stage[a].astype(F32) for a in range(4)], axis=0).astype(BF16)
    for h in range(nu):
        sbuf[h] = packed[:, h * D : (h + 1) * D]
    rbuf[0] = sbuf[head]

    pl.semaphore_wait(barrier, len(partners))

    for i in range(nu - 1, 0, -1):
        remote(
            sbuf.at[flipped(head, head_flip, i)], rbuf.at[i], a2a_send, a2a_recv, h_mask(i)
        ).start()
    pltpu.make_async_copy(
        rbuf.at[pl.ds(0, nu - 1)], rbuf.at[pl.ds(0, nu - 1)], a2a_recv
    ).wait()

    piece = GROUP * t
    for m in range(nu // GROUP):
        x = rbuf[m * GROUP : (m + 1) * GROUP].reshape(GROUP * pack, D)
        s = jnp.dot(sort_ref[...], x, preferred_element_type=F32).astype(BF16)
        lo, hi = m * piece, (m + 1) * piece
        qg[0, 0, lo:hi, :] = s[0:piece]
        kv[0, 0, lo:hi, :] = s[piece : 2 * piece]
        kv[1, 0, lo:hi, :] = s[2 * piece : 3 * piece]
        qg[1, 0, lo:hi, :] = s[3 * piece : 4 * piece]

    def q_slot(a, k):
        return qg.at[a, k // 2, pl.ds((k % 2) * rows, rows)]

    sends = []

    def q_go(a, src, step):
        k = src ^ step
        c = remote(
            q_slot(a, src), q_slot(a, k), qg_ssem.at[a, k], qg_rsem.at[a, k], q_mask(step)
        )
        c.start()
        sends.append(c)

    def k_go(a, src, step):
        j = src ^ step
        c = remote(
            kv.at[a, src], kv.at[a, j], kv_ssem.at[a, j], kv_rsem.at[a, j], k_mask(step)
        )
        c.start()
        sends.append(c)

    def q_wait(a, k):
        pltpu.make_async_copy(q_slot(a, k), q_slot(a, k), qg_rsem.at[a, k]).wait()

    def k_wait(a, j):
        pltpu.make_async_copy(kv.at[a, j], kv.at[a, j], kv_rsem.at[a, j]).wait()

    def tile(p, j):
        s = dot_nt(kv[0, j], qg[0, p]) * scale2
        m = jnp.max(s, axis=0, keepdims=True)
        e = jnp.exp2(s - m)
        gw = dot_nt(kv[1, j], qg[1, p])
        e_s[j, p] = e
        gw_s[j, p] = gw
        mlr[j, p, 0:1] = m
        mlr[j, p, 1:2] = jnp.sum(e, axis=0, keepdims=True)
        mlr[j, p, 2:3] = jnp.sum(e * gw, axis=0, keepdims=True)

    def tiles(ps, js):
        n = len(js)

        def step(i, carry):
            tile(ps[0] + i // n, js[0] + i % n)
            return carry

        lax.fori_loop(0, len(ps) * n, step, 0)

    def statistics(p):
        ms = [mlr[j, p, 0:1] for j in range(NK)]
        top = functools.reduce(jnp.maximum, ms)
        fs = [jnp.exp2(m - top) for m in ms]
        tot = sum(mlr[j, p, 1:2] * fs[j] for j in range(NK))
        dot = sum(mlr[j, p, 2:3] * fs[j] for j in range(NK))
        for n, val in enumerate((top + log2(tot), dot / tot)):
            st_send[0, p, n : n + 1] = val
            st_send[1, p, n : n + 1] = jnp.concatenate([val[:, rows:], val[:, :rows]], axis=1)

    def statistics_go(first, count, n):
        for k in range(1, NQ):
            part = pl.ds(first, count)
            remote(
                st_send.at[k % 2, part], st_all.at[k, part], st_ssem.at[n], st_rsem.at[n],
                q_mask(k),
            ).start()

    for a in (0, 1):
        k_go(a, 0, 2)
        q_go(a, 0, 2)
    for a in (0, 1):
        q_go(a, 0, 4)
        k_go(a, 0, 1)
    for a in (0, 1):
        q_go(a, 0, 1)
    for a in (0, 1):
        q_wait(a, 2)
        q_go(a, 2, 4)
        q_go(a, 2, 1)
        k_wait(a, 2)
        k_go(a, 2, 1)
    for a in (0, 1):
        q_wait(a, 1)
    tiles((0,), (0,))
    for a in (0, 1):
        q_wait(a, 4)
        q_go(a, 4, 1)
    for a in (0, 1):
        k_wait(a, 1)
    tiles((0,), (1, 2))
    for a in (0, 1):
        q_wait(a, 6)
        q_go(a, 6, 1)
    for a in (0, 1):
        q_wait(a, 3)
        q_wait(a, 5)
    tiles((1, 2), (0, 1, 2))
    for a in (0, 1):
        k_wait(a, 3)
    tiles((0, 1, 2), (3,))
    for p in range(NP - 1):
        statistics(p)
    statistics_go(0, NP - 1, 0)
    for a in (0, 1):
        q_wait(a, 7)
    tiles((3,), (0, 1, 2, 3))
    statistics(NP - 1)
    statistics_go(NP - 1, 1, 1)

    st_all[0] = st_send[0]
    keys_t = jnp.concatenate([kv[0, j].astype(F32).T for j in range(NK)], axis=1).astype(BF16)
    early, late = st_all.at[pl.ds(0, NQ - 1), pl.ds(0, NP - 1)], st_all.at[pl.ds(0, NQ - 1), pl.ds(0, 1)]
    pltpu.make_async_copy(early, early, st_rsem.at[0]).wait()
    pltpu.make_async_copy(late, late, st_rsem.at[1]).wait()
    for p in range(NP):
        got = [st_all[k, p ^ (k >> 1)] for k in range(NQ)]
        tops = [x[0:1] for x in got]
        top = functools.reduce(jnp.maximum, tops)
        total = top + log2(sum(jnp.exp2(x - top) for x in tops))
        fin[p, 0:1] = total
        fin[p, 1:2] = sum(jnp.exp2(x[0:1] - total) * x[1:2] for x in got)

    for j in (3, 2, 1, 0):
        dk = jnp.zeros((rows, D), F32)
        dv = jnp.zeros((rows, D), F32)
        for p in range(NP):
            w = e_s[j, p] * jnp.exp2(mlr[j, p, 0:1] - fin[p, 0:1])
            gl = (w * (gw_s[j, p] - fin[p, 1:2])).astype(BF16)
            gl_s[j, p] = gl
            dv = dv + jnp.dot(w.astype(BF16), qg[1, p], preferred_element_type=F32)
            dk = dk + jnp.dot(gl, qg[0, p], preferred_element_type=F32)
        buf = dkv_send if j else dkv_recv
        buf[j, 0] = (dk * scale).astype(BF16)
        buf[j, 1] = dv.astype(BF16)
        if j:
            remote(dkv_send.at[j], dkv_recv.at[j], dkv_ssem, dkv_rsem, k_mask(j)).start()

    for p in (3, 2, 1, 0):
        gl = jnp.concatenate([gl_s[j, p] for j in range(NK)], axis=0)
        dq = (jnp.dot(keys_t, gl, preferred_element_type=F32) * scale).T.astype(BF16)
        for k in (2 * p + 1, 2 * p):
            part = dq[(k % 2) * rows : (k % 2 + 1) * rows]
            if k:
                dq_send[k] = part
                remote(dq_send.at[k], dq_recv.at[k], dq_ssem, dq_rsem, q_mask(k)).start()
            else:
                dq_recv[0] = part

    pltpu.make_async_copy(
        dkv_recv.at[pl.ds(0, NK - 1)], dkv_recv.at[pl.ds(0, NK - 1)], dkv_rsem
    ).wait()
    dk = sum(dkv_recv[j, 0].astype(F32) for j in range(NK)).astype(BF16)
    dv = sum(dkv_recv[j, 1].astype(F32) for j in range(NK)).astype(BF16)
    pltpu.make_async_copy(
        dq_recv.at[pl.ds(0, NQ - 1)], dq_recv.at[pl.ds(0, NQ - 1)], dq_rsem
    ).wait()
    dq = sum(dq_recv[k].astype(F32) for k in range(NQ)).astype(BF16)

    for m in range(nu // GROUP):
        lo, hi = m * piece, (m + 1) * piece
        x = jnp.concatenate([dq[lo:hi], dk[lo:hi], dv[lo:hi]], axis=0)
        s = jnp.dot(unsort_ref[...], x, preferred_element_type=F32).astype(BF16)
        osend[m * GROUP : (m + 1) * GROUP] = s.reshape(GROUP, pack, D)
    for i in range(nu - 1, 0, -1):
        remote(osend.at[i], orecv.at[head], out_send, out_recv, h_mask(i)).start()
    orecv[head] = osend[0]
    pltpu.make_async_copy(
        orecv.at[pl.ds(0, nu - 1)], orecv.at[pl.ds(0, nu - 1)], out_recv
    ).wait()
    for h in range(nu):
        x = orecv[h].astype(F32)
        dq_ref[:, h * D : (h + 1) * D] = x[0:t].astype(BF16)
        dk_ref[:, h * D : (h + 1) * D] = x[t : 2 * t].astype(BF16)
        dv_ref[:, h * D : (h + 1) * D] = x[2 * t : 3 * t].astype(BF16)

    for view, sem in (
        (sbuf.at[pl.ds(0, nu - 1)], a2a_send), (early, st_ssem.at[0]), (late, st_ssem.at[1]),
        (dkv_send.at[pl.ds(0, NK - 1)], dkv_ssem), (dq_send.at[pl.ds(0, NQ - 1)], dq_ssem),
        (osend.at[pl.ds(0, nu - 1)], out_send),
    ):
        pltpu.make_async_copy(view, view, sem).wait()
    for c in sends:
        c.wait_send()


def sort_matrices(t):
    n = GROUP * t
    sort = np.zeros((4 * n, 4 * n), np.float32)
    for a in range(4):
        for g in range(GROUP):
            for i in range(t):
                sort[a * n + g * t + i, g * 4 * t + a * t + i] = 1.0
    return jnp.asarray(sort, BF16), jnp.asarray(sort[: 3 * n].T, BF16)


def local(nu, queries, key_vectors, value_vectors, cotangent):
    t = queries.shape[0]
    rows = nu * t
    cols = 2 * rows
    sort, unsort = sort_matrices(t)
    vmem = pl.BlockSpec(memory_space=pltpu.VMEM)
    hbm = pl.BlockSpec(memory_space=pltpu.HBM)
    out = jax.ShapeDtypeStruct(queries.shape, BF16)
    dma = pltpu.SemaphoreType.DMA
    args = [
        pltpu.with_memory_space_constraint(x, pltpu.HBM)
        for x in (queries, key_vectors, value_vectors, cotangent, sort, unsort)
    ]
    return pl.pallas_call(
        functools.partial(kernel, nu, t),
        out_shape=(out, out, out),
        in_specs=[hbm] * 6,
        out_specs=(vmem, vmem, vmem),
        scratch_shapes=[
            pltpu.VMEM((4, *queries.shape), BF16),
            pltpu.VMEM(sort.shape, BF16),
            pltpu.VMEM(unsort.shape, BF16),
            pltpu.VMEM((nu, 4 * t, D), BF16),
            pltpu.VMEM((nu, 4 * t, D), BF16),
            pltpu.VMEM((2, NP, cols, D), BF16),
            pltpu.VMEM((2, NK, rows, D), BF16),
            pltpu.VMEM((NK, NP, rows, cols), F32),
            pltpu.VMEM((NK, NP, rows, cols), F32),
            pltpu.VMEM((NK, NP, rows, cols), BF16),
            pltpu.VMEM((NK, NP, 8, cols), F32),
            pltpu.VMEM((NP, 8, cols), F32),
            pltpu.VMEM((2, NP, 2, cols), F32),
            pltpu.VMEM((NQ, NP, 2, cols), F32),
            pltpu.VMEM((NQ, rows, D), BF16),
            pltpu.VMEM((NQ, rows, D), BF16),
            pltpu.VMEM((NK, 2, rows, D), BF16),
            pltpu.VMEM((NK, 2, rows, D), BF16),
            pltpu.VMEM((nu, 4 * t, D), BF16),
            pltpu.VMEM((nu, 4 * t, D), BF16),
            dma((4,)), dma((2,)), dma, dma,
            dma((2, NK)), dma((2, NK)), dma((2, NQ)), dma((2, NQ)),
            dma((2,)), dma((2,)), dma, dma, dma, dma, dma, dma,
        ],
        compiler_params=pltpu.CompilerParams(
            collective_id=0, has_side_effects=True, vmem_limit_bytes=48 << 20
        ),
    )(*args)


def solution(mesh):
    placed = P(("blk", "ulysses"), None)
    return jax.shard_map(
        functools.partial(local, mesh.shape["ulysses"]),
        mesh=mesh,
        in_specs=(placed,) * 4,
        out_specs=(placed,) * 3,
        check_vma=False,
    )
```

time: 732 us -> 74.3 us (0.10)
  the two profiles are of different devices: /device:TPU:1 before, /device:TPU:2 now
where the time goes in v1:
time: 74.3 us; the launch traced here: 74.1 us
  Pallas kernels  71.6 us (96%)
  local copies, waits for them, and re-layouts  1.89 us (3%)
    pallas_call x1, Pallas kernels, local(): pl.pallas_call(functools.partial(kernel, nu, t), out_shape=(out, out, out...  71.6 us
    unnamed x3, local copies, waits for them, and re-layouts  1.89 us

profile of v1, /device:TPU:2, one launch (start us, length us, event | category | flops | bytes accessed | tf_op | source)
XLA Modules:
  0.0 74.1 jit_solution(2464686171995122145)
XLA Ops:
  0.6 71.6 %shard_map.85 = (bf16[6,4096]{1,0:T(8,128)(2,1)S(1)}, bf16[6,4096]{1,0:T(8,128)(2,1)S(1)}, bf16[6,4096]{1,0:T(8,128)(2,1)S(1)}) custom-call(bf16[6,4096]{1,0:T(8,128)(2,1)} %q_hbm.1, bf16[6,4096]{1,0:T(8,128)(2,1)} %k_hbm.1, bf16[6,4096]{1,0:T(8,128)(2,1)} %v_hbm.1, bf16[6,4096]{1,0:T(8,128)(2,1)} %g_hbm.1, bf16[192,192]{1,0:T(8,128)(2,1)} %constant.4.clone.sort_hbm, ...), custom_call_target="tpu_custom_call" | custom-call | tf_op jit(solution)/shard_map/pallas_call | solution.py:331
  72.2 0.6 copy.12
  72.9 0.6 copy.13
  73.5 0.6 copy.14

commit v2 on v1

--- a/solution.py
+++ b/solution.py
@@ -36,7 +36,7 @@
 
 def h_mask(i):
     iz, ix, iy = i >> 4, (i >> 2) & 3, i & 3
-    mb = iy << 3 | (4 if iy == 2 else 0) | (3 if iz else 0)
+    mb = iy << 3 | (4 if iy == 2 else 0) | (2 if iz else 0)
     mu = iz << 4 | ix << 2 | (2 if ix == 2 else 0)
     return mb, mu
 
@@ -44,7 +44,7 @@
 def kernel(
     nu, t, q_hbm, k_hbm, v_hbm, g_hbm, sort_hbm, unsort_hbm, dq_ref, dk_ref, dv_ref,
     stage, sort_ref, unsort_ref, sbuf, rbuf, qg, kv, e_s, gw_s, gl_s, mlr, fin, st_send, st_all,
-    dq_send, dq_recv, dkv_send, dkv_recv, osend, orecv,
+    dq_send, dq_recv, dq_part, dq_own, dkv_send, dkv_recv, dkv_own, osend, orecv,
     stage_sem, sort_sem, a2a_send, a2a_recv, kv_ssem, kv_rsem, qg_ssem, qg_rsem,
     st_ssem, st_rsem, dq_ssem, dq_rsem, dkv_ssem, dkv_rsem, out_send, out_recv,
 ):
@@ -242,7 +242,7 @@
         fin[p, 0:1] = total
         fin[p, 1:2] = sum(jnp.exp2(x[0:1] - total) * x[1:2] for x in got)
 
-    for j in (3, 2, 1, 0):
+    for j in (3, 1, 2, 0):
         dk = jnp.zeros((rows, D), F32)
         dv = jnp.zeros((rows, D), F32)
         for p in range(NP):
@@ -251,38 +251,68 @@
             gl_s[j, p] = gl
             dv = dv + jnp.dot(w.astype(BF16), qg[1, p], preferred_element_type=F32)
             dk = dk + jnp.dot(gl, qg[0, p], preferred_element_type=F32)
-        buf = dkv_send if j else dkv_recv
-        buf[j, 0] = (dk * scale).astype(BF16)
-        buf[j, 1] = dv.astype(BF16)
-        if j:
-            remote(dkv_send.at[j], dkv_recv.at[j], dkv_ssem, dkv_rsem, k_mask(j)).start()
+        if j % 2:
+            dkv_send[j, 0] = (dk * scale).astype(BF16)
+            dkv_send[j, 1] = dv.astype(BF16)
+            c = remote(
+                dkv_send.at[j], dkv_recv.at[j ^ 1], dkv_ssem.at[j], dkv_rsem.at[j ^ 1], k_mask(1)
+            )
+            c.start()
+            sends.append(c)
+        else:
+            dkv_own[j // 2, 0] = dk * scale
+            dkv_own[j // 2, 1] = dv
 
     for p in (3, 2, 1, 0):
         gl = jnp.concatenate([gl_s[j, p] for j in range(NK)], axis=0)
-        dq = (jnp.dot(keys_t, gl, preferred_element_type=F32) * scale).T.astype(BF16)
-        for k in (2 * p + 1, 2 * p):
-            part = dq[(k % 2) * rows : (k % 2 + 1) * rows]
+        dq = (jnp.dot(keys_t, gl, preferred_element_type=F32) * scale).T
+        if p >= 2:
+            dq_send[p] = dq.astype(BF16)
+            c = remote(
+                dq_send.at[p], dq_recv.at[p - 2], dq_ssem.at[p], dq_rsem.at[p - 2], q_mask(4)
+            )
+            c.start()
+            sends.append(c)
+        else:
+            dq_own[p] = dq
+
+    def landed(ref, sem):
+        pltpu.make_async_copy(ref, ref, sem).wait()
+
+    landed(dkv_recv.at[2], dkv_rsem.at[2])
+    dkv_send[2] = (dkv_own[1] + dkv_recv[2].astype(F32)).astype(BF16)
+    c = remote(dkv_send.at[2], dkv_recv.at[1], dkv_ssem.at[2], dkv_rsem.at[1], k_mask(2))
+    c.start()
+    sends.append(c)
+    for p in (1, 0):
+        landed(dq_recv.at[p], dq_rsem.at[p])
+        dq = dq_own[p] + dq_recv[p].astype(F32)
+        dq_send[p] = dq.astype(BF16)
+        for k in (2 * p, 2 * p + 1):
             if k:
-                dq_send[k] = part
-                remote(dq_send.at[k], dq_recv.at[k], dq_ssem, dq_rsem, q_mask(k)).start()
-            else:
-                dq_recv[0] = part
-
-    pltpu.make_async_copy(
-        dkv_recv.at[pl.ds(0, NK - 1)], dkv_recv.at[pl.ds(0, NK - 1)], dkv_rsem
-    ).wait()
-    dk = sum(dkv_recv[j, 0].astype(F32) for j in range(NK)).astype(BF16)
-    dv = sum(dkv_recv[j, 1].astype(F32) for j in range(NK)).astype(BF16)
-    pltpu.make_async_copy(
-        dq_recv.at[pl.ds(0, NQ - 1)], dq_recv.at[pl.ds(0, NQ - 1)], dq_rsem
-    ).wait()
-    dq = sum(dq_recv[k].astype(F32) for k in range(NQ)).astype(BF16)
+                part = pl.ds((k % 2) * rows, rows)
+                c = remote(
+                    dq_send.at[p, part], dq_part.at[k], dq_ssem.at[3 + k], dq_rsem.at[1 + k],
+                    q_mask(k),
+                )
+                c.start()
+                sends.append(c)
+    dq = dq[:rows]
+    landed(dkv_recv.at[0], dkv_rsem.at[0])
+    dkv = dkv_own[0] + dkv_recv[0].astype(F32)
+    for k in (1, 2, 3):
+        landed(dq_part.at[k], dq_rsem.at[1 + k])
+        dq = dq + dq_part[k].astype(F32)
+    dq = dq.astype(BF16)
+    landed(dkv_recv.at[1], dkv_rsem.at[1])
+    dkv = (dkv + dkv_recv[1].astype(F32)).astype(BF16)
+    dk, dv = dkv[0], dkv[1]
 
     for m in range(nu // GROUP):
         lo, hi = m * piece, (m + 1) * piece
         x = jnp.concatenate([dq[lo:hi], dk[lo:hi], dv[lo:hi]], axis=0)
         s = jnp.dot(unsort_ref[...], x, preferred_element_type=F32).astype(BF16)
-        osend[m * GROUP : (m + 1) * GROUP] = s.reshape(GROUP, pack, D)
+        osend[m * GROUP : (m + 1) * GROUP] = s.reshape(GROUP, pack, D)[:, : 3 * t]
     for i in range(nu - 1, 0, -1):
         remote(osend.at[i], orecv.at[head], out_send, out_recv, h_mask(i)).start()
     orecv[head] = osend[0]
@@ -297,7 +327,6 @@
 
     for view, sem in (
         (sbuf.at[pl.ds(0, nu - 1)], a2a_send), (early, st_ssem.at[0]), (late, st_ssem.at[1]),
-        (dkv_send.at[pl.ds(0, NK - 1)], dkv_ssem), (dq_send.at[pl.ds(0, NQ - 1)], dq_ssem),
         (osend.at[pl.ds(0, nu - 1)], out_send),
     ):
         pltpu.make_async_copy(view, view, sem).wait()
@@ -348,15 +377,18 @@
             pltpu.VMEM((NP, 8, cols), F32),
             pltpu.VMEM((2, NP, 2, cols), F32),
             pltpu.VMEM((NQ, NP, 2, cols), F32),
-            pltpu.VMEM((NQ, rows, D), BF16),
-            pltpu.VMEM((NQ, rows, D), BF16),
+            pltpu.VMEM((NP, cols, D), BF16),
+            pltpu.VMEM((2, cols, D), BF16),
+            pltpu.VMEM((4, rows, D), BF16),
+            pltpu.VMEM((2, cols, D), F32),
             pltpu.VMEM((NK, 2, rows, D), BF16),
-            pltpu.VMEM((NK, 2, rows, D), BF16),
-            pltpu.VMEM((nu, 4 * t, D), BF16),
-            pltpu.VMEM((nu, 4 * t, D), BF16),
+            pltpu.VMEM((3, 2, rows, D), BF16),
+            pltpu.VMEM((2, 2, rows, D), F32),
+            pltpu.VMEM((nu, 3 * t, D), BF16),
+            pltpu.VMEM((nu, 3 * t, D), BF16),
             dma((4,)), dma((2,)), dma, dma,
             dma((2, NK)), dma((2, NK)), dma((2, NQ)), dma((2, NQ)),
-            dma((2,)), dma((2,)), dma, dma, dma, dma, dma, dma,
+            dma((2,)), dma((2,)), dma((8,)), dma((8,)), dma((4,)), dma((4,)), dma, dma,
         ],
         compiler_params=pltpu.CompilerParams(
             collective_id=0, has_side_effects=True, vmem_limit_bytes=48 << 20

time: 74.3 us -> 74.5 us (level)
  no operation moved by 1% of the time
where the time goes in v2:
time: 74.5 us; the launch traced here: 74.1 us
  Pallas kernels  71.5 us (96%)
  local copies, waits for them, and re-layouts  1.89 us (3%)
    pallas_call x1, Pallas kernels, local(): pl.pallas_call(functools.partial(kernel, nu, t), out_shape=(out, out, out...  71.5 us
    unnamed x3, local copies, waits for them, and re-layouts  1.89 us

profile of v2, /device:TPU:2, one launch (start us, length us, event | category | flops | bytes accessed | tf_op | source)
XLA Modules:
  0.0 74.1 jit_solution(9738970757846562113)
XLA Ops:
  0.6 71.5 %shard_map.85 = (bf16[6,4096]{1,0:T(8,128)(2,1)S(1)}, bf16[6,4096]{1,0:T(8,128)(2,1)S(1)}, bf16[6,4096]{1,0:T(8,128)(2,1)S(1)}) custom-call(bf16[6,4096]{1,0:T(8,128)(2,1)} %q_hbm.1, bf16[6,4096]{1,0:T(8,128)(2,1)} %k_hbm.1, bf16[6,4096]{1,0:T(8,128)(2,1)} %v_hbm.1, bf16[6,4096]{1,0:T(8,128)(2,1)} %g_hbm.1, bf16[192,192]{1,0:T(8,128)(2,1)} %constant.4.clone.sort_hbm, ...), custom_call_target="tpu_custom_call" | custom-call | tf_op jit(solution)/shard_map/pallas_call | solution.py:360
  72.2 0.6 copy.12
  72.8 0.6 copy.13
  73.4 0.6 copy.14

commit v3 on v2

--- a/solution.py
+++ b/solution.py
@@ -44,7 +44,7 @@
 def kernel(
     nu, t, q_hbm, k_hbm, v_hbm, g_hbm, sort_hbm, unsort_hbm, dq_ref, dk_ref, dv_ref,
     stage, sort_ref, unsort_ref, sbuf, rbuf, qg, kv, e_s, gw_s, gl_s, mlr, fin, st_send, st_all,
-    dq_send, dq_recv, dq_part, dq_own, dkv_send, dkv_recv, dkv_own, osend, orecv,
+    dq_send, dq_recv, dq_part, dq_own, dkv_send, dkv_recv, dkv_own, dkv_acc, osend, orecv,
     stage_sem, sort_sem, a2a_send, a2a_recv, kv_ssem, kv_rsem, qg_ssem, qg_rsem,
     st_ssem, st_rsem, dq_ssem, dq_rsem, dkv_ssem, dkv_rsem, out_send, out_recv,
 ):
@@ -78,6 +78,14 @@
             device_id=peer(masks), device_id_type=pl.DeviceIdType.MESH,
         )
 
+    barrier = pltpu.get_barrier_semaphore()
+    partners = [h_mask(i) for i in range(nu - 1, 0, -1)]
+    partners += [q_mask(k) for k in range(1, NQ)] + [k_mask(j) for j in range(1, NK)]
+    for masks in partners:
+        pl.semaphore_signal(
+            barrier, inc=1, device_id=peer(masks), device_id_type=pl.DeviceIdType.MESH
+        )
+
     loads = [
         pltpu.make_async_copy(src, stage.at[a], stage_sem.at[a])
         for a, src in enumerate((q_hbm, k_hbm, v_hbm, g_hbm))
@@ -87,14 +95,6 @@
     for c in loads:
         c.start()
 
-    barrier = pltpu.get_barrier_semaphore()
-    partners = [h_mask(i) for i in range(1, nu)]
-    partners += [q_mask(k) for k in range(1, NQ)] + [k_mask(j) for j in range(1, NK)]
-    for masks in partners:
-        pl.semaphore_signal(
-            barrier, inc=1, device_id=peer(masks), device_id_type=pl.DeviceIdType.MESH
-        )
-
     for c in loads:
         c.wait()
     packed = jnp.concatenate([stage[a].astype(F32) for a in range(4)], axis=0).astype(BF16)
@@ -106,14 +106,18 @@
 
     for i in range(nu - 1, 0, -1):
         remote(
-            sbuf.at[flipped(head, head_flip, i)], rbuf.at[i], a2a_send, a2a_recv, h_mask(i)
+            sbuf.at[flipped(head, head_flip, i)], rbuf.at[i], a2a_send,
+            a2a_recv.at[i // GROUP], h_mask(i),
         ).start()
-    pltpu.make_async_copy(
-        rbuf.at[pl.ds(0, nu - 1)], rbuf.at[pl.ds(0, nu - 1)], a2a_recv
-    ).wait()
+
+    def group_wait(buf, sem, m):
+        first = max(m * GROUP, 1)
+        part = buf.at[pl.ds(first, (m + 1) * GROUP - first)]
+        pltpu.make_async_copy(part, part, sem.at[m]).wait()
 
     piece = GROUP * t
     for m in range(nu // GROUP):
+        group_wait(rbuf, a2a_recv, m)
         x = rbuf[m * GROUP : (m + 1) * GROUP].reshape(GROUP * pack, D)
         s = jnp.dot(sort_ref[...], x, preferred_element_type=F32).astype(BF16)
         lo, hi = m * piece, (m + 1) * piece
@@ -180,7 +184,7 @@
             st_send[1, p, n : n + 1] = jnp.concatenate([val[:, rows:], val[:, :rows]], axis=1)
 
     def statistics_go(first, count, n):
-        for k in range(1, NQ):
+        for k in range(NQ - 1, 0, -1):
             part = pl.ds(first, count)
             remote(
                 st_send.at[k % 2, part], st_all.at[k, part], st_ssem.at[n], st_rsem.at[n],
@@ -188,8 +192,8 @@
             ).start()
 
     for a in (0, 1):
+        q_go(a, 0, 2)
         k_go(a, 0, 2)
-        q_go(a, 0, 2)
     for a in (0, 1):
         q_go(a, 0, 4)
         k_go(a, 0, 1)
@@ -242,15 +246,29 @@
         fin[p, 0:1] = total
         fin[p, 1:2] = sum(jnp.exp2(x[0:1] - total) * x[1:2] for x in got)
 
-    for j in (3, 1, 2, 0):
-        dk = jnp.zeros((rows, D), F32)
-        dv = jnp.zeros((rows, D), F32)
-        for p in range(NP):
+    def adjoint(j, ps, dk, dv):
+        for p in ps:
             w = e_s[j, p] * jnp.exp2(mlr[j, p, 0:1] - fin[p, 0:1])
             gl = (w * (gw_s[j, p] - fin[p, 1:2])).astype(BF16)
             gl_s[j, p] = gl
             dv = dv + jnp.dot(w.astype(BF16), qg[1, p], preferred_element_type=F32)
             dk = dk + jnp.dot(gl, qg[0, p], preferred_element_type=F32)
+        return dk, dv
+
+    def query_adjoint(p):
+        gl = jnp.concatenate([gl_s[j, p] for j in range(NK)], axis=0)
+        return (jnp.dot(keys_t, gl, preferred_element_type=F32) * scale).T
+
+    for j in range(NK):
+        zero = jnp.zeros((rows, D), F32)
+        dkv_acc[j, 0], dkv_acc[j, 1] = adjoint(j, (3, 2), zero, zero)
+    for p in (3, 2):
+        dq_send[p] = query_adjoint(p).astype(BF16)
+        c = remote(dq_send.at[p], dq_recv.at[p - 2], dq_ssem.at[p], dq_rsem.at[p - 2], q_mask(4))
+        c.start()
+        sends.append(c)
+    for j in (3, 1, 2, 0):
+        dk, dv = adjoint(j, (1, 0), dkv_acc[j, 0], dkv_acc[j, 1])
         if j % 2:
             dkv_send[j, 0] = (dk * scale).astype(BF16)
             dkv_send[j, 1] = dv.astype(BF16)
@@ -262,19 +280,8 @@
         else:
             dkv_own[j // 2, 0] = dk * scale
             dkv_own[j // 2, 1] = dv
-
-    for p in (3, 2, 1, 0):
-        gl = jnp.concatenate([gl_s[j, p] for j in range(NK)], axis=0)
-        dq = (jnp.dot(keys_t, gl, preferred_element_type=F32) * scale).T
-        if p >= 2:
-            dq_send[p] = dq.astype(BF16)
-            c = remote(
-                dq_send.at[p], dq_recv.at[p - 2], dq_ssem.at[p], dq_rsem.at[p - 2], q_mask(4)
-            )
-            c.start()
-            sends.append(c)
-        else:
-            dq_own[p] = dq
+    for p in (1, 0):
+        dq_own[p] = query_adjoint(p)
 
     def landed(ref, sem):
         pltpu.make_async_copy(ref, ref, sem).wait()
@@ -308,22 +315,22 @@
     dkv = (dkv + dkv_recv[1].astype(F32)).astype(BF16)
     dk, dv = dkv[0], dkv[1]
 
-    for m in range(nu // GROUP):
+    for m in range(nu // GROUP - 1, -1, -1):
         lo, hi = m * piece, (m + 1) * piece
         x = jnp.concatenate([dq[lo:hi], dk[lo:hi], dv[lo:hi]], axis=0)
         s = jnp.dot(unsort_ref[...], x, preferred_element_type=F32).astype(BF16)
         osend[m * GROUP : (m + 1) * GROUP] = s.reshape(GROUP, pack, D)[:, : 3 * t]
-    for i in range(nu - 1, 0, -1):
-        remote(osend.at[i], orecv.at[head], out_send, out_recv, h_mask(i)).start()
-    orecv[head] = osend[0]
-    pltpu.make_async_copy(
-        orecv.at[pl.ds(0, nu - 1)], orecv.at[pl.ds(0, nu - 1)], out_recv
-    ).wait()
-    for h in range(nu):
-        x = orecv[h].astype(F32)
-        dq_ref[:, h * D : (h + 1) * D] = x[0:t].astype(BF16)
-        dk_ref[:, h * D : (h + 1) * D] = x[t : 2 * t].astype(BF16)
-        dv_ref[:, h * D : (h + 1) * D] = x[2 * t : 3 * t].astype(BF16)
+        for i in range((m + 1) * GROUP - 1, max(m * GROUP, 1) - 1, -1):
+            remote(osend.at[i], orecv.at[i], out_send, out_recv.at[m], h_mask(i)).start()
+    orecv[0] = osend[0]
+    for m in range(nu // GROUP):
+        group_wait(orecv, out_recv, m)
+        for i in range(m * GROUP, (m + 1) * GROUP):
+            at = pl.ds(pl.multiple_of(flipped(head, head_flip, i) * D, D), D)
+            x = orecv[i].astype(F32)
+            dq_ref[:, at] = x[0:t].astype(BF16)
+            dk_ref[:, at] = x[t : 2 * t].astype(BF16)
+            dv_ref[:, at] = x[2 * t : 3 * t].astype(BF16)
 
     for view, sem in (
         (sbuf.at[pl.ds(0, nu - 1)], a2a_send), (early, st_ssem.at[0]), (late, st_ssem.at[1]),
@@ -384,11 +391,12 @@
             pltpu.VMEM((NK, 2, rows, D), BF16),
             pltpu.VMEM((3, 2, rows, D), BF16),
             pltpu.VMEM((2, 2, rows, D), F32),
+            pltpu.VMEM((NK, 2, rows, D), F32),
             pltpu.VMEM((nu, 3 * t, D), BF16),
             pltpu.VMEM((nu, 3 * t, D), BF16),
-            dma((4,)), dma((2,)), dma, dma,
+            dma((4,)), dma((2,)), dma, dma((nu // GROUP,)),
             dma((2, NK)), dma((2, NK)), dma((2, NQ)), dma((2, NQ)),
-            dma((2,)), dma((2,)), dma((8,)), dma((8,)), dma((4,)), dma((4,)), dma, dma,
+            dma((2,)), dma((2,)), dma((8,)), dma((8,)), dma((4,)), dma((4,)), dma, dma((nu // GROUP,)),
         ],
         compiler_params=pltpu.CompilerParams(
             collective_id=0, has_side_effects=True, vmem_limit_bytes=48 << 20

time: 74.5 us -> 73.7 us (0.989)
  no operation moved by 1% of the time
where the time goes in v3:
time: 73.7 us; the launch traced here: 73.5 us
  Pallas kernels  71 us (96%)
  local copies, waits for them, and re-layouts  1.89 us (3%)
    pallas_call x1, Pallas kernels, local(): pl.pallas_call(functools.partial(kernel, nu, t), out_shape=(out, out, out...  71 us
    unnamed x3, local copies, waits for them, and re-layouts  1.89 us

profile of v3, /device:TPU:2, one launch (start us, length us, event | category | flops | bytes accessed | tf_op | source)
XLA Modules:
  0.0 73.5 jit_solution(15906304000906134131)
XLA Ops:
  0.6 71.0 %shard_map.85 = (bf16[6,4096]{1,0:T(8,128)(2,1)S(1)}, bf16[6,4096]{1,0:T(8,128)(2,1)S(1)}, bf16[6,4096]{1,0:T(8,128)(2,1)S(1)}) custom-call(bf16[6,4096]{1,0:T(8,128)(2,1)} %q_hbm.1, bf16[6,4096]{1,0:T(8,128)(2,1)} %k_hbm.1, bf16[6,4096]{1,0:T(8,128)(2,1)} %v_hbm.1, bf16[6,4096]{1,0:T(8,128)(2,1)} %g_hbm.1, bf16[192,192]{1,0:T(8,128)(2,1)} %constant.4.clone.sort_hbm, ...), custom_call_target="tpu_custom_call" | custom-call | tf_op jit(solution)/shard_map/pallas_call | solution.py:367
  71.6 0.6 copy.12
  72.3 0.6 copy.13
  72.9 0.6 copy.14

commit v4 on v3

--- a/solution.py
+++ b/solution.py
@@ -42,7 +42,7 @@
 
 
 def kernel(
-    nu, t, q_hbm, k_hbm, v_hbm, g_hbm, sort_hbm, unsort_hbm, dq_ref, dk_ref, dv_ref,
+    nu, t, q_hbm, k_hbm, v_hbm, g_hbm, sort_hbm, unsort_hbm, out_ref,
     stage, sort_ref, unsort_ref, sbuf, rbuf, qg, kv, e_s, gw_s, gl_s, mlr, fin, st_send, st_all,
     dq_send, dq_recv, dq_part, dq_own, dkv_send, dkv_recv, dkv_own, dkv_acc, osend, orecv,
     stage_sem, sort_sem, a2a_send, a2a_recv, kv_ssem, kv_rsem, qg_ssem, qg_rsem,
@@ -139,10 +139,16 @@
         c.start()
         sends.append(c)
 
-    def k_go(a, src, step):
-        j = src ^ step
+    def k_slot(a, j, half):
+        if half is None:
+            return kv.at[a, j]
+        return kv.at[a, j, pl.ds(half * (rows // 2), rows // 2)]
+
+    def k_go(a, src, step, half=None):
+        j, n = src ^ step, half or 0
         c = remote(
-            kv.at[a, src], kv.at[a, j], kv_ssem.at[a, j], kv_rsem.at[a, j], k_mask(step)
+            k_slot(a, src, half), k_slot(a, j, half), kv_ssem.at[a, j, n], kv_rsem.at[a, j, n],
+            k_mask(step),
         )
         c.start()
         sends.append(c)
@@ -150,8 +156,9 @@
     def q_wait(a, k):
         pltpu.make_async_copy(q_slot(a, k), q_slot(a, k), qg_rsem.at[a, k]).wait()
 
-    def k_wait(a, j):
-        pltpu.make_async_copy(kv.at[a, j], kv.at[a, j], kv_rsem.at[a, j]).wait()
+    def k_wait(a, j, half=None):
+        part = k_slot(a, j, half)
+        pltpu.make_async_copy(part, part, kv_rsem.at[a, j, half or 0]).wait()
 
     def tile(p, j):
         s = dot_nt(kv[0, j], qg[0, p]) * scale2
@@ -193,7 +200,8 @@
 
     for a in (0, 1):
         q_go(a, 0, 2)
-        k_go(a, 0, 2)
+        for half in (0, 1):
+            k_go(a, 0, 2, half)
     for a in (0, 1):
         q_go(a, 0, 4)
         k_go(a, 0, 1)
@@ -203,8 +211,9 @@
         q_wait(a, 2)
         q_go(a, 2, 4)
         q_go(a, 2, 1)
-        k_wait(a, 2)
-        k_go(a, 2, 1)
+        for half in (0, 1):
+            k_wait(a, 2, half)
+            k_go(a, 2, 1, half)
     for a in (0, 1):
         q_wait(a, 1)
     tiles((0,), (0,))
@@ -222,7 +231,8 @@
         q_wait(a, 5)
     tiles((1, 2), (0, 1, 2))
     for a in (0, 1):
-        k_wait(a, 3)
+        for half in (0, 1):
+            k_wait(a, 3, half)
     tiles((0, 1, 2), (3,))
     for p in range(NP - 1):
         statistics(p)
@@ -328,9 +338,9 @@
         for i in range(m * GROUP, (m + 1) * GROUP):
             at = pl.ds(pl.multiple_of(flipped(head, head_flip, i) * D, D), D)
             x = orecv[i].astype(F32)
-            dq_ref[:, at] = x[0:t].astype(BF16)
-            dk_ref[:, at] = x[t : 2 * t].astype(BF16)
-            dv_ref[:, at] = x[2 * t : 3 * t].astype(BF16)
+            out_ref[0, :, at] = x[0:t].astype(BF16)
+            out_ref[1, :, at] = x[t : 2 * t].astype(BF16)
+            out_ref[2, :, at] = x[2 * t : 3 * t].astype(BF16)
 
     for view, sem in (
         (sbuf.at[pl.ds(0, nu - 1)], a2a_send), (early, st_ssem.at[0]), (late, st_ssem.at[1]),
@@ -358,17 +368,17 @@
     sort, unsort = sort_matrices(t)
     vmem = pl.BlockSpec(memory_space=pltpu.VMEM)
     hbm = pl.BlockSpec(memory_space=pltpu.HBM)
-    out = jax.ShapeDtypeStruct(queries.shape, BF16)
+    out = jax.ShapeDtypeStruct((3, *queries.shape), BF16)
     dma = pltpu.SemaphoreType.DMA
     args = [
         pltpu.with_memory_space_constraint(x, pltpu.HBM)
         for x in (queries, key_vectors, value_vectors, cotangent, sort, unsort)
     ]
-    return pl.pallas_call(
+    grads = pl.pallas_call(
         functools.partial(kernel, nu, t),
-        out_shape=(out, out, out),
+        out_shape=out,
         in_specs=[hbm] * 6,
-        out_specs=(vmem, vmem, vmem),
+        out_specs=vmem,
         scratch_shapes=[
             pltpu.VMEM((4, *queries.shape), BF16),
             pltpu.VMEM(sort.shape, BF16),
@@ -395,13 +405,14 @@
             pltpu.VMEM((nu, 3 * t, D), BF16),
             pltpu.VMEM((nu, 3 * t, D), BF16),
             dma((4,)), dma((2,)), dma, dma((nu // GROUP,)),
-            dma((2, NK)), dma((2, NK)), dma((2, NQ)), dma((2, NQ)),
+            dma((2, NK, 2)), dma((2, NK, 2)), dma((2, NQ)), dma((2, NQ)),
             dma((2,)), dma((2,)), dma((8,)), dma((8,)), dma((4,)), dma((4,)), dma, dma((nu // GROUP,)),
         ],
         compiler_params=pltpu.CompilerParams(
             collective_id=0, has_side_effects=True, vmem_limit_bytes=48 << 20
         ),
     )(*args)
+    return grads[0], grads[1], grads[2]
 
 
 def solution(mesh):

time: 73.7 us -> 72.6 us (0.985)
  local copies, waits for them, and re-layouts: 1.89 us -> 0.68 us
    unnamed x3 -> x0, local copies, waits for them, and re-layouts: 1.89 us -> none
where the time goes in v4:
time: 72.6 us; the launch traced here: 72.4 us
  Pallas kernels  71.1 us (98%)
    pallas_call x1, Pallas kernels, local(): pl.pallas_call(functools.partial(kernel, nu, t), out_shape=out, in_specs=...  71.1 us

profile of v4, /device:TPU:2, one launch (start us, length us, event | category | flops | bytes accessed | tf_op | source)
XLA Modules:
  0.0 72.4 jit_solution(17607789198620637869)
XLA Ops:
  0.6 71.1 %shard_map.85 = bf16[3,6,4096]{2,1,0:T(8,128)(2,1)S(1)} custom-call(bf16[6,4096]{1,0:T(8,128)(2,1)} %q_hbm.1, bf16[6,4096]{1,0:T(8,128)(2,1)} %k_hbm.1, bf16[6,4096]{1,0:T(8,128)(2,1)} %v_hbm.1, bf16[6,4096]{1,0:T(8,128)(2,1)} %g_hbm.1, bf16[192,192]{1,0:T(8,128)(2,1)} %constant.4.clone.sort_hbm, bf16[192,144]{1,0:T(8,128)(2,1)} %constant.5.clone.unsort_hbm), custom_call_target="tpu_custom_call" | custom-call | tf_op jit(solution)/shard_map/pallas_call | solution.py:377
  71.8 0.7 slice_bitcast_fusion

commit v5 on v4

--- a/solution.py
+++ b/solution.py
@@ -265,6 +265,14 @@
             dk = dk + jnp.dot(gl, qg[0, p], preferred_element_type=F32)
         return dk, dv
 
+    def dkv_go(a, src, dst, step):
+        c = remote(
+            dkv_send.at[src, a], dkv_recv.at[dst, a], dkv_ssem.at[a, src], dkv_rsem.at[a, dst],
+            k_mask(step),
+        )
+        c.start()
+        sends.append(c)
+
     def query_adjoint(p):
         gl = jnp.concatenate([gl_s[j, p] for j in range(NK)], axis=0)
         return (jnp.dot(keys_t, gl, preferred_element_type=F32) * scale).T
@@ -282,11 +290,8 @@
         if j % 2:
             dkv_send[j, 0] = (dk * scale).astype(BF16)
             dkv_send[j, 1] = dv.astype(BF16)
-            c = remote(
-                dkv_send.at[j], dkv_recv.at[j ^ 1], dkv_ssem.at[j], dkv_rsem.at[j ^ 1], k_mask(1)
-            )
-            c.start()
-            sends.append(c)
+            for a in (0, 1):
+                dkv_go(a, j, j ^ 1, 1)
         else:
             dkv_own[j // 2, 0] = dk * scale
             dkv_own[j // 2, 1] = dv
@@ -296,11 +301,10 @@
     def landed(ref, sem):
         pltpu.make_async_copy(ref, ref, sem).wait()
 
-    landed(dkv_recv.at[2], dkv_rsem.at[2])
-    dkv_send[2] = (dkv_own[1] + dkv_recv[2].astype(F32)).astype(BF16)
-    c = remote(dkv_send.at[2], dkv_recv.at[1], dkv_ssem.at[2], dkv_rsem.at[1], k_mask(2))
-    c.start()
-    sends.append(c)
+    for a in (0, 1):
+        landed(dkv_recv.at[2, a], dkv_rsem.at[a, 2])
+        dkv_send[2, a] = (dkv_own[1, a] + dkv_recv[2, a].astype(F32)).astype(BF16)
+        dkv_go(a, 2, 1, 2)
     for p in (1, 0):
         landed(dq_recv.at[p], dq_rsem.at[p])
         dq = dq_own[p] + dq_recv[p].astype(F32)
@@ -315,13 +319,15 @@
                 c.start()
                 sends.append(c)
     dq = dq[:rows]
-    landed(dkv_recv.at[0], dkv_rsem.at[0])
+    for a in (0, 1):
+        landed(dkv_recv.at[0, a], dkv_rsem.at[a, 0])
     dkv = dkv_own[0] + dkv_recv[0].astype(F32)
     for k in (1, 2, 3):
         landed(dq_part.at[k], dq_rsem.at[1 + k])
         dq = dq + dq_part[k].astype(F32)
     dq = dq.astype(BF16)
-    landed(dkv_recv.at[1], dkv_rsem.at[1])
+    for a in (0, 1):
+        landed(dkv_recv.at[1, a], dkv_rsem.at[a, 1])
     dkv = (dkv + dkv_recv[1].astype(F32)).astype(BF16)
     dk, dv = dkv[0], dkv[1]
 
@@ -406,7 +412,7 @@
             pltpu.VMEM((nu, 3 * t, D), BF16),
             dma((4,)), dma((2,)), dma, dma((nu // GROUP,)),
             dma((2, NK, 2)), dma((2, NK, 2)), dma((2, NQ)), dma((2, NQ)),
-            dma((2,)), dma((2,)), dma((8,)), dma((8,)), dma((4,)), dma((4,)), dma, dma((nu // GROUP,)),
+            dma((2,)), dma((2,)), dma((8,)), dma((8,)), dma((2, 4)), dma((2, 4)), dma, dma((nu // GROUP,)),
         ],
         compiler_params=pltpu.CompilerParams(
             collective_id=0, has_side_effects=True, vmem_limit_bytes=48 << 20

time: 72.6 us -> 72.1 us (level)
  no operation moved by 1% of the time
where the time goes in v5:
time: 72.1 us; the launch traced here: 71.9 us
  Pallas kernels  70.6 us (98%)
    pallas_call x1, Pallas kernels, local(): pl.pallas_call(functools.partial(kernel, nu, t), out_shape=out, in_specs=...  70.6 us

profile of v5, /device:TPU:2, one launch (start us, length us, event | category | flops | bytes accessed | tf_op | source)
XLA Modules:
  0.0 71.9 jit_solution(11974261940674075860)
XLA Ops:
  0.6 70.6 %shard_map.85 = bf16[3,6,4096]{2,1,0:T(8,128)(2,1)S(1)} custom-call(bf16[6,4096]{1,0:T(8,128)(2,1)} %q_hbm.1, bf16[6,4096]{1,0:T(8,128)(2,1)} %k_hbm.1, bf16[6,4096]{1,0:T(8,128)(2,1)} %v_hbm.1, bf16[6,4096]{1,0:T(8,128)(2,1)} %g_hbm.1, bf16[192,192]{1,0:T(8,128)(2,1)} %constant.4.clone.sort_hbm, bf16[192,144]{1,0:T(8,128)(2,1)} %constant.5.clone.unsort_hbm), custom_call_target="tpu_custom_call" | custom-call | tf_op jit(solution)/shard_map/pallas_call | solution.py:383
  71.3 0.7 slice_bitcast_fusion
